TPU v7x, 128 devices: a whole 4x4x4 slice. The times are simulated.
128 devices in a mesh: gz: 16 (over z, x), gx: 8 (over y, core).
Axes of the slice: x: 4, y: 4, z: 4, core: 2. Of those that a mesh axis runs over, the one named last changes fastest.
Arguments:
- atom_velocity: float32 [3, 16384, 128], P(None, ('gz', 'gx')), may hold values from -4.2 to 4.2
- atom_noise: float32 [3, 16384, 128], P(None, ('gz', 'gx')), may hold values from -6 to 6
- atom_plane: int32 [16384, 128], P(('gz', 'gx')), may hold values from 0 to 255, as said below
- atom_column: int32 [16384, 128], P(('gz', 'gx')), may hold values from 0 to 4095
- brick_count: int32 [16384], P(('gz', 'gx')), may hold values from 32 to 128, as said below
- electron_temp: float32 [256, 128, 256], P('gz', 'gx'), may hold values from 0.05 to 3.8
Outputs:
- new_temp: float32 [256, 128, 256], P('gz', 'gx')
- new_velocity: float32 [3, 16384, 128], P(None, ('gz', 'gx'))
Inputs may be any that keep to these rules, and one draw needn't show every extreme that they name: `atom_plane`: all 128 entries of a brick lie in one slab of 16 planes (the planes of one gz index). No slab holds more than 16 bricks of one device, and in every draw one slab holds exactly 16 bricks of every device. `brick_count`: every device holds a brick with 128 used slots.
All inputs are finite; a program needn't handle non-finite values.
Results may differ from a plain program's by a relative error of at most 0.00035.
Values sent between devices are 32-bit elements; how exact they have to be, the bound alone decides.
A program may use at most 128 MiB of HBM per device.

v0:
```python
import jax
import jax.numpy as jnp
from jax import lax
from jax.experimental import pallas as pl
from jax.experimental.pallas import tpu as pltpu
from jax.sharding import PartitionSpec as P

STIFFNESS = 10000.0
LATERAL = 0.1
COUPLE = 0.5
TWO_THIRDS = 2.0 / 3.0
KICK_RATE = 0.2
SLABS = 16
PLANES = 16
WIDTH = 16
NY = 256
SLOTS = 16
BRICKS = 128
LANES = 128
F32 = jnp.float32
BF16 = jnp.bfloat16
VMEM = pl.BlockSpec(memory_space=pltpu.VMEM)


def iota(shape, axis):
    return lax.broadcasted_iota(jnp.int32, shape, axis)


def split3(value):
    high = value.astype(BF16)
    rest = value - high.astype(F32)
    middle = rest.astype(BF16)
    low = (rest - middle.astype(F32)).astype(BF16)
    return high, middle, low


def split2(value):
    high = value.astype(BF16)
    low = (value - high.astype(F32)).astype(BF16)
    return high, low


def dot(a, b, contract=((1,), (0,))):
    return lax.dot_general(a, b, (contract, ((), ())), preferred_element_type=F32)


def used_mask(count_row):
    diagonal = iota((BRICKS, LANES), 0) == iota((BRICKS, LANES), 1)
    count_column = jnp.sum(jnp.where(diagonal, count_row.astype(F32), 0.0), axis=1, keepdims=True)
    return iota((BRICKS, LANES), 1).astype(F32) < count_column


def prep_kernel(velocity, plane, column, count, send, slot):
    used = used_mask(count[...])
    speed = velocity[...]
    kinetic = 0.5 * (speed[0] * speed[0] + speed[1] * speed[1] + speed[2] * speed[2])
    kinetic = jnp.where(used, kinetic, 0.0)
    planes = plane[...]
    columns = column[...]
    owner = planes[:, 0:1] // PLANES
    square = (BRICKS, LANES)
    hits = jnp.where(iota(square, 1) == owner, 1.0, 0.0)
    earlier = jnp.where(iota(square, 0) > iota(square, 1), 1.0, 0.0).astype(BF16)
    before = dot(earlier, hits.astype(BF16))
    rank = jnp.sum(before * hits, axis=1, keepdims=True)
    brick_slot = owner.astype(F32) * SLOTS + rank
    slot[...] = jnp.broadcast_to(brick_slot, square)
    slot_row = jnp.sum(
        jnp.where(iota(square, 0) == iota(square, 1), brick_slot, 0.0), axis=0, keepdims=True
    )
    slots = SLABS * SLOTS
    pick = jnp.where(iota((slots, BRICKS), 0).astype(F32) == slot_row, 1.0, 0.0).astype(BF16)
    row_code = (planes - owner * PLANES) * WIDTH + columns // NY + 1
    row_code = jnp.where(used, row_code, 0).astype(F32).astype(BF16)
    y_code = jnp.where(used, columns % NY, 0).astype(F32).astype(BF16)
    code = 256.0 * dot(pick, row_code) + dot(pick, y_code)
    high, middle, low = split3(kinetic)
    sent = (dot(pick, high) + dot(pick, middle)) + dot(pick, low)
    send[:, 0] = sent.reshape(SLABS, SLOTS, LANES)
    send[:, 1] = code.reshape(SLABS, SLOTS, LANES)


ROWS = PLANES * WIDTH


def bin_chunk(kinetic, code):
    whole = code.astype(jnp.int32)
    row = ((whole // 256) - 1).astype(F32)
    y = (whole % 256).astype(F32)
    high = kinetic.astype(BF16).astype(F32)
    low = kinetic - high
    row_ids = iota((ROWS, LANES), 0).astype(F32).astype(BF16)
    y_ids = row_ids
    one = jnp.ones((), BF16)
    zero = jnp.zeros((), BF16)
    left = []
    right = []
    for brick in range(SLOTS):
        at = slice(brick, brick + 1)

        def spread(value):
            return jnp.broadcast_to(value[at], (ROWS, LANES)).astype(BF16)

        hit = row_ids == spread(row)
        left.append(
            jnp.concatenate(
                [
                    jnp.where(hit, spread(high), zero),
                    jnp.where(hit, spread(low), zero),
                    jnp.where(hit, one, zero),
                ],
                axis=0,
            )
        )
        right.append(jnp.where(y_ids == spread(y), one, zero))
    return dot(
        jnp.concatenate(left, axis=1), jnp.concatenate(right, axis=1), contract=((1,), (1,))
    )


def bin_kernel(got, temp, below, left, right, reduced, fixed, to_low, to_high, totals):
    totals[...] = jnp.zeros_like(totals)

    def chunk(source, carry):
        totals[...] += bin_chunk(got[source, 0], got[source, 1])
        return carry

    lax.fori_loop(0, SLABS, chunk, 0)
    slab = lax.axis_index("gz")
    has_below = jnp.where(slab > 0, 1.0, 0.0)
    shape = (WIDTH, NY)
    lower = has_below * (STIFFNESS * (0.5 * (temp[0] + below[0])))
    ground = current = link = back_ground = back_current = None
    for p in range(PLANES):
        here = temp[p]
        rows = slice(p * WIDTH, (p + 1) * WIDTH)
        energy = totals[rows] + totals[ROWS + p * WIDTH : ROWS + (p + 1) * WIDTH]
        count = totals[2 * ROWS + p * WIDTH : 2 * ROWS + (p + 1) * WIDTH]
        x_less = jnp.concatenate([left[p], here[:-1]], axis=0)
        x_more = jnp.concatenate([here[1:], right[p]], axis=0)
        y_less = pltpu.roll(here, 1, 1)
        y_more = pltpu.roll(here, NY - 1, 1)
        lateral = LATERAL * (x_less + x_more + y_less + y_more - 4.0 * here)
        excess = here + COUPLE * count
        source = here * here + lateral + (COUPLE * TWO_THIRDS) * energy
        if p == 0:
            link, ground, current = lower, excess, source
            back_ground = back_current = jnp.zeros(shape, F32)
        else:
            upper = STIFFNESS * (0.5 * (temp[p - 1] + here))
            inverse = 1.0 / (ground + link + upper)
            high = upper * inverse
            low = link * inverse
            fixed[p - 1] = current * inverse
            to_low[p - 1] = low
            to_high[p - 1] = high
            back_ground = back_ground + low * ground
            back_current = back_current + low * current
            link = high * link
            ground = excess + high * ground
            current = source + high * current
    for place, value in enumerate([link, ground, current, back_ground, back_current]):
        reduced[:, place, :] = value


def shift_rows(value, step):
    zeros = jnp.zeros((abs(step), value.shape[1]), value.dtype)
    if step > 0:
        return jnp.concatenate([value[step:], zeros], axis=0)
    return jnp.concatenate([zeros, value[:step]], axis=0)


def reduce_kernel(got, ends):
    link, ground, current, back_ground, back_current = [got[:, place, :] for place in range(5)]
    ground = ground + shift_rows(back_ground, 1)
    current = current + shift_rows(back_current, 1)
    below = link
    above = shift_rows(link, 1)
    distance = 1
    while distance < SLABS:
        inverse = 1.0 / (ground + below + above)
        ratio_below = below * shift_rows(inverse, -distance)
        ratio_above = above * shift_rows(inverse, distance)
        ground, current, below, above = (
            ground
            + ratio_below * shift_rows(ground, -distance)
            + ratio_above * shift_rows(ground, distance),
            current
            + ratio_below * shift_rows(current, -distance)
            + ratio_above * shift_rows(current, distance),
            ratio_below * shift_rows(below, -distance),
            ratio_above * shift_rows(above, distance),
        )
        distance *= 2
    value = current / ground
    ends[:, 0, :] = shift_rows(value, -1)
    ends[:, 1, :] = value


def look_chunk(table_high, table_low, code):
    whole = code.astype(jnp.int32)
    row = ((whole // 256) - 1).astype(F32)
    y = (whole % 256).astype(F32)
    y_ids = iota((NY, LANES), 0).astype(F32).astype(BF16)
    row_ids = iota((ROWS, LANES), 0).astype(F32)
    one = jnp.ones((), BF16)
    zero = jnp.zeros((), BF16)
    right = []
    for brick in range(SLOTS):
        spread = jnp.broadcast_to(y[brick : brick + 1], (NY, LANES)).astype(BF16)
        right.append(jnp.where(y_ids == spread, one, zero))
    hot = jnp.concatenate(right, axis=1)
    picked = dot(table_high, hot) + dot(table_low, hot)
    out = []
    for brick in range(SLOTS):
        part = picked[:, brick * LANES : (brick + 1) * LANES]
        hit = row_ids == jnp.broadcast_to(row[brick : brick + 1], (ROWS, LANES))
        out.append(jnp.sum(jnp.where(hit, part, 0.0), axis=0, keepdims=True))
    return jnp.concatenate(out, axis=0)


def back_kernel(fixed, to_low, to_high, ends, got, solved, reply, high_table, low_table):
    low_end = ends[:, 0, :]
    value = ends[:, 1, :]
    for p in range(PLANES - 1, -1, -1):
        if p < PLANES - 1:
            value = (fixed[p] + to_low[p] * low_end) + to_high[p] * value
        solved[p] = value
        high, low = split2(value)
        high_table[p * WIDTH : (p + 1) * WIDTH] = high
        low_table[p * WIDTH : (p + 1) * WIDTH] = low

    def chunk(source, carry):
        reply[source] = look_chunk(high_table[...], low_table[...], got[source, 1])
        return carry

    lax.fori_loop(0, SLABS, chunk, 0)


def kick_kernel(velocity, noise, count, slot, returned, moved):
    used = used_mask(count[...])
    slots = SLABS * SLOTS
    slot_ids = iota((BRICKS, slots), 1).astype(F32)
    where_from = jnp.concatenate([slot[...], slot[...]], axis=1)
    pick = jnp.where(slot_ids == where_from, 1.0, 0.0).astype(BF16)
    high, middle, low = split3(returned[...].reshape(slots, LANES))
    temp = (dot(pick, high) + dot(pick, middle)) + dot(pick, low)
    scale = jnp.sqrt(2.0 * KICK_RATE * temp)
    for axis in range(3):
        kicked = (1.0 - KICK_RATE) * velocity[axis] + scale * noise[axis]
        moved[axis] = jnp.where(used, kicked, 0.0)


def shape(*dims):
    return jax.ShapeDtypeStruct(dims, F32)


def call(kernel, count, outs, scratch=(), **params):
    return pl.pallas_call(
        kernel,
        out_shape=outs,
        in_specs=[VMEM] * count,
        out_specs=jax.tree.map(lambda _: VMEM, outs),
        scratch_shapes=list(scratch),
        compiler_params=pltpu.CompilerParams(**params),
    )


def ring(value, axis, step, closed):
    size = lax.axis_size(axis)
    pairs = [(i, (i + step) % size) for i in range(size) if closed or 0 <= i + step < size]
    return lax.ppermute(value, axis, pairs)


def body(velocity, noise, plane, column, brick_count, temp):
    count = brick_count.reshape(1, BRICKS)
    below = ring(temp[-1:], "gz", 1, False)
    left = ring(temp[:, -1:], "gx", 1, True)
    right = ring(temp[:, :1], "gx", -1, True)
    send, slot = call(
        prep_kernel, 4, (shape(SLABS, 2, SLOTS, LANES), shape(BRICKS, LANES))
    )(velocity, plane, column, count)
    got = lax.all_to_all(send, "gz", 0, 0, tiled=True)
    inner = shape(PLANES - 1, WIDTH, NY)
    reduced, fixed, to_low, to_high = call(
        bin_kernel,
        5,
        (shape(WIDTH, 5, NY), inner, inner, inner),
        [pltpu.VMEM((3 * ROWS, NY), F32)],
    )(got, temp, below, left, right)
    systems = lax.all_to_all(reduced, "gz", 0, 0, tiled=True)
    ends = call(reduce_kernel, 1, shape(SLABS, 2, NY))(systems)
    own_ends = lax.all_to_all(ends, "gz", 0, 0, tiled=True)
    solved, reply = call(
        back_kernel,
        5,
        (shape(PLANES, WIDTH, NY), shape(SLABS, SLOTS, LANES)),
        [pltpu.VMEM((ROWS, NY), BF16)] * 2,
    )(fixed, to_low, to_high, own_ends, got)
    returned = lax.all_to_all(reply, "gz", 0, 0, tiled=True)
    moved = call(kick_kernel, 5, shape(3, BRICKS, LANES))(velocity, noise, count, slot, returned)
    return solved, moved


def solution(mesh):
    placed = (
        P(None, ("gz", "gx"), None),
        P(None, ("gz", "gx"), None),
        P(("gz", "gx"), None),
        P(("gz", "gx"), None),
        P(("gz", "gx")),
        P("gz", "gx", None),
    )
    return jax.shard_map(
        body,
        mesh=mesh,
        in_specs=placed,
        out_specs=(P("gz", "gx", None), P(None, ("gz", "gx"), None)),
        check_vma=False,
    )
```

profile of v0, /device:TPU:0, one launch (start us, length us, event | category | flops | bytes accessed | tf_op | source)
XLA Modules:
  0.0 98.4 jit_solution(7552417831532969526)
XLA Ops:
  0.6 2.3 %shard_map.77 = (f32[16,2,16,128]{3,2,1,0:T(8,128)}, f32[128,128]{1,0:T(8,128)}) custom-call(f32[3,128,128]{2,1,0:T(8,128)} %velocity.3, s32[128,128]{1,0:T(8,128)} %plane.1, s32[128,128]{1,0:T(8,128)} %column.1, s32[1,128]{1,0:T(1,128)} %bitcast.1), custom_call_target="tpu_custom_call" | custom-call | tf_op jit(solution)/shard_map/pallas_call | solution.py:280
  2.9 8.0 %all-to-all-start = ((f32[16,2,16,128]{3,2,1,0:T(8,128)}), f32[16,2,16,128]{3,2,1,0:T(8,128)S(1)}, u32[]{:S(2)}, u32[]{:S(2)}) async-start(f32[16,2,16,128]{3,2,1,0:T(8,128)} %get-tuple-element.10), calls=%async_computation | async-start | bytes 524288 | tf_op jit(solution)/shard_map/all_to_all | solution.py:283
  10.9 0.7 slice.9
  11.6 3.8 %collective-permute-start = (f32[1,16,256]{2,1,0:T(8,128)S(1)}, f32[1,16,256]{2,1,0:T(8,128)S(1)}, u32[]{:S(2)}, u32[]{:S(2)}) collective-permute-start(f32[1,16,256]{2,1,0:T(8,128)S(1)} %slice.9), channel_id=1, source_target_pairs={{0,8},{8,16},{16,24},{24,32},{32,40},{40,48},{48,56},{56,64},{64,7... | collective-permute-start | bytes 49160 | tf_op jit(solution)/shard_map/ppermute | solution.py:272
  15.5 1.0 %fusion = (f32[16,1,256]{2,1,0:T(1,128)S(1)}, f32[16,1,256]{2,1,0:T(1,128)S(1)}) fusion(f32[16,16,256]{2,1,0:T(8,128)} %temp.1), kind=kLoop, calls=%fused_computation | loop fusion | bytes 65536 | tf_op jit(solution)/shard_map/slice | solution.py:279
  16.5 1.6 %collective-permute-start.2 = (f32[16,1,256]{2,1,0:T(1,128)S(1)}, f32[16,1,256]{2,1,0:T(1,128)S(1)}, u32[]{:S(2)}, u32[]{:S(2)}) collective-permute-start(f32[16,1,256]{2,1,0:T(1,128)S(1)} %get-tuple-element.18), channel_id=1, source_target_pairs={{0,7},{1,0},{2,1},{3,2},{4,3},{5,4},{6,5},{7,6},{8,15},{9,8},{10,9... | collective-permute-start | bytes 49160 | tf_op jit(solution)/shard_map/ppermute | solution.py:272
  18.1 0.0 collective-permute-start.1
  18.1 0.0 collective-permute-done.below
  18.1 0.0 copy-start.1
  18.1 1.4 %collective-permute-done.2.right = f32[16,1,256]{2,1,0:T(1,128)S(1)} collective-permute-done((f32[16,1,256]{2,1,0:T(1,128)S(1)}, f32[16,1,256]{2,1,0:T(1,128)S(1)}, u32[]{:S(2)}, u32[]{:S(2)}) %collective-permute-start.2) | collective-permute-done | bytes 16416 | tf_op jit(solution)/shard_map/ppermute | solution.py:272
  19.5 0.0 copy-start.2
  19.5 2.9 %collective-permute-done.1.left = f32[16,1,256]{2,1,0:T(1,128)S(1)} collective-permute-done((f32[16,1,256]{2,1,0:T(1,128)S(1)}, f32[16,1,256]{2,1,0:T(1,128)S(1)}, u32[]{:S(2)}, u32[]{:S(2)}) %collective-permute-start.1) | collective-permute-done | bytes 16416 | tf_op jit(solution)/shard_map/ppermute | solution.py:272
  22.5 0.0 copy-start.3
  22.5 0.0 all-to-all-done.got
  22.5 0.0 copy-done.1
  22.5 0.0 copy-done.2
  22.5 0.6 copy-done.3
  23.1 0.0 copy-start
  23.1 0.7 copy-done
  23.8 18.7 %shard_map.78 = (f32[16,5,256]{2,1,0:T(8,128)}, f32[15,16,256]{2,1,0:T(8,128)}, f32[15,16,256]{2,1,0:T(8,128)}, f32[15,16,256]{2,1,0:T(8,128)}) custom-call(f32[16,2,16,128]{3,2,1,0:T(8,128)} %copy-done, f32[16,16,256]{2,1,0:T(8,128)} %temp.1, f32[1,16,256]{2,1,0:T(8,128)} %copy-done.1, f32[16,1,256]{2,1,0:T(1,128)} %copy-done.3, f32[16,1,256]{2,1,0:T(1,128)} %copy-done.2), custom_call_target="tpu_custom_call" | custom-call | tf_op jit(solution)/shard_map/pallas_call | solution.py:285
  42.5 14.6 %all_to_all.20.got = f32[16,5,256]{2,1,0:T(8,128)} all-to-all(f32[16,5,256]{2,1,0:T(8,128)} %get-tuple-element.14), channel_id=1, replica_groups=mesh['gz'=16,'gx'=8] {'gz'}, dimensions={0} | all-to-all | bytes 163840 | tf_op jit(solution)/shard_map/all_to_all | solution.py:291
  57.0 1.6 %shard_map.79 = f32[16,2,256]{2,1,0:T(2,128)} custom-call(f32[16,5,256]{2,1,0:T(8,128)} %all_to_all.20.got), custom_call_target="tpu_custom_call" | custom-call | tf_op jit(solution)/shard_map/pallas_call | solution.py:292
  58.7 11.7 %all_to_all.21.ends = f32[16,2,256]{2,1,0:T(2,128)} all-to-all(f32[16,2,256]{2,1,0:T(2,128)} %shard_map.79), channel_id=1, replica_groups=mesh['gz'=16,'gx'=8] {'gz'}, dimensions={0} | all-to-all | bytes 65536 | tf_op jit(solution)/shard_map/all_to_all | solution.py:293
  70.4 13.8 %shard_map.80 = (f32[16,16,256]{2,1,0:T(8,128)}, f32[16,16,128]{2,1,0:T(8,128)}) custom-call(f32[15,16,256]{2,1,0:T(8,128)} %get-tuple-element.11.fixed, f32[15,16,256]{2,1,0:T(8,128)} %get-tuple-element.12.to_low, f32[15,16,256]{2,1,0:T(8,128)} %get-tuple-element.13.to_high, f32[16,2,256]{2,1,0:T(2,128)} %all_to_all.21.ends, f32[16,2,16,128]{3,2,1,0:T(8,128)} %copy-done), custom_call_target="tpu_custom_call" | custom-call | tf_op jit(solution)/shard_map/pallas_call | solution.py:294
  84.2 12.2 %all_to_all.22.returned = f32[16,16,128]{2,1,0:T(8,128)} all-to-all(f32[16,16,128]{2,1,0:T(8,128)} %get-tuple-element.17), channel_id=1, replica_groups=mesh['gz'=16,'gx'=8] {'gz'}, dimensions={0} | all-to-all | bytes 262144 | tf_op jit(solution)/shard_map/all_to_all | solution.py:300
  96.4 2.1 %shard_map.81 = f32[3,128,128]{2,1,0:T(8,128)} custom-call(f32[3,128,128]{2,1,0:T(8,128)} %velocity.3, f32[3,128,128]{2,1,0:T(8,128)} %noise.1, s32[1,128]{1,0:T(1,128)} %bitcast.2, f32[128,128]{1,0:T(8,128)} %get-tuple-element.16.slot, f32[16,16,128]{2,1,0:T(8,128)} %all_to_all.22.returned), custom_call_target="tpu_custom_call" | custom-call | tf_op jit(solution)/shard_map/pallas_call | solution.py:301
Async XLA Ops:
  2.9 19.5 %all-to-all-start = ((f32[16,2,16,128]{3,2,1,0:T(8,128)}), f32[16,2,16,128]{3,2,1,0:T(8,128)S(1)}, u32[]{:S(2)}, u32[]{:S(2)}) async-start(f32[16,2,16,128]{3,2,1,0:T(8,128)} %get-tuple-element.10), calls=%async_computation | async-start | bytes 524288 | tf_op jit(solution)/shard_map/all_to_all | solution.py:283
  11.6 6.5 %collective-permute-start = (f32[1,16,256]{2,1,0:T(8,128)S(1)}, f32[1,16,256]{2,1,0:T(8,128)S(1)}, u32[]{:S(2)}, u32[]{:S(2)}) collective-permute-start(f32[1,16,256]{2,1,0:T(8,128)S(1)} %slice.9), channel_id=1, source_target_pairs={{0,8},{8,16},{16,24},{24,32},{32,40},{40,48},{48,56},{56,64},{64,7... | collective-permute-start | bytes 49160 | tf_op jit(solution)/shard_map/ppermute | solution.py:272
  16.5 3.1 %collective-permute-start.2 = (f32[16,1,256]{2,1,0:T(1,128)S(1)}, f32[16,1,256]{2,1,0:T(1,128)S(1)}, u32[]{:S(2)}, u32[]{:S(2)}) collective-permute-start(f32[16,1,256]{2,1,0:T(1,128)S(1)} %get-tuple-element.18), channel_id=1, source_target_pairs={{0,7},{1,0},{2,1},{3,2},{4,3},{5,4},{6,5},{7,6},{8,15},{9,8},{10,9... | collective-permute-start | bytes 49160 | tf_op jit(solution)/shard_map/ppermute | solution.py:272
  18.1 4.4 %collective-permute-start.1 = (f32[16,1,256]{2,1,0:T(1,128)S(1)}, f32[16,1,256]{2,1,0:T(1,128)S(1)}, u32[]{:S(2)}, u32[]{:S(2)}) collective-permute-start(f32[16,1,256]{2,1,0:T(1,128)S(1)} %get-tuple-element.19), channel_id=1, source_target_pairs={{0,1},{1,2},{2,3},{3,4},{4,5},{5,6},{6,7},{7,0},{8,9},{9,10},{10,1... | collective-permute-start | bytes 49160 | tf_op jit(solution)/shard_map/ppermute | solution.py:272
  18.1 4.4 %copy-start.1 = (f32[1,16,256]{2,1,0:T(8,128)}, f32[1,16,256]{2,1,0:T(8,128)S(1)}, u32[]{:S(2)}) copy-start(f32[1,16,256]{2,1,0:T(8,128)S(1)} %collective-permute-done.below) | copy-start | bytes 49156
  19.5 2.9 %copy-start.2 = (f32[16,1,256]{2,1,0:T(1,128)}, f32[16,1,256]{2,1,0:T(1,128)S(1)}, u32[]{:S(2)}) copy-start(f32[16,1,256]{2,1,0:T(1,128)S(1)} %collective-permute-done.2.right) | copy-start | bytes 49156
  22.5 0.6 copy-start.3
  23.1 0.7 copy-start
where the time goes:
time: 99 us; the launch traced here: 98.4 us
  Pallas kernels  38.5 us (39%)
  blocking collectives  38.4 us (39%)
  starting transfers between devices  13.4 us (14%)
  waiting for transfers between devices  4.37 us (4%)
  local copies, waits for them, and re-layouts  3.02 us (3%)
    pallas_call x1, Pallas kernels, body(): call(bin_kernel, 5, (shape(WIDTH, 5, NY), inner, inner, inner), [pltpu.VM...  18.7 us
    all_to_all x1, blocking collectives, body(): systems = lax.all_to_all(reduced, 'gz', 0, 0, tiled=True)  14.6 us
    pallas_call x1, Pallas kernels, body(): call(back_kernel, 5, (shape(PLANES, WIDTH, NY), shape(SLABS, SLOTS, LANES...  13.8 us
    all_to_all x1, blocking collectives, body(): returned = lax.all_to_all(reply, 'gz', 0, 0, tiled=True)  12.2 us
    all_to_all x1, blocking collectives, body(): own_ends = lax.all_to_all(ends, 'gz', 0, 0, tiled=True)  11.7 us
    all_to_all x1, starting transfers between devices, body(): got = lax.all_to_all(send, 'gz', 0, 0, tiled=True)  7.99 us
    ppermute x3, starting transfers between devices, ring(): return lax.ppermute(value, axis, pairs)  5.44 us
    ppermute x3, waiting for transfers between devices, ring(): return lax.ppermute(value, axis, pairs)  4.36 us
  transfers between devices with their start and end apart: 4, of which 2 were waited for; matrix products, arithmetic and copies ran while one was open for 2% of the time, Pallas kernels for 0%

commit v1 on v0

v1 whole, which is shorter than its diff:
```python
import jax
import jax.numpy as jnp
from jax import lax
from jax.experimental import pallas as pl
from jax.experimental.pallas import tpu as pltpu
from jax.sharding import PartitionSpec as P

STIFFNESS = 10000.0
LATERAL = 0.1
COUPLE = 0.5
TWO_THIRDS = 2.0 / 3.0
KICK_RATE = 0.2
SLABS = 16
PLANES = 16
WIDTH = 16
NY = 256
SLOTS = 16
BRICKS = 128
LANES = 128
F32 = jnp.float32
BF16 = jnp.bfloat16
VMEM = pl.BlockSpec(memory_space=pltpu.VMEM)


def iota(shape, axis):
    return lax.broadcasted_iota(jnp.int32, shape, axis)


def split3(value):
    high = value.astype(BF16)
    rest = value - high.astype(F32)
    middle = rest.astype(BF16)
    low = (rest - middle.astype(F32)).astype(BF16)
    return high, middle, low


def split2(value):
    high = value.astype(BF16)
    low = (value - high.astype(F32)).astype(BF16)
    return high, low


def dot(a, b, contract=((1,), (0,))):
    return lax.dot_general(a, b, (contract, ((), ())), preferred_element_type=F32)


def used_mask(count_row):
    diagonal = iota((BRICKS, LANES), 0) == iota((BRICKS, LANES), 1)
    count_column = jnp.sum(jnp.where(diagonal, count_row.astype(F32), 0.0), axis=1, keepdims=True)
    return iota((BRICKS, LANES), 1).astype(F32) < count_column


ROWS = PLANES * WIDTH


def bin_chunk(kinetic, code):
    whole = code.astype(jnp.int32)
    row = ((whole // 256) - 1).astype(F32)
    y = (whole % 256).astype(F32)
    high = kinetic.astype(BF16).astype(F32)
    low = kinetic - high
    row_ids = iota((ROWS, LANES), 0).astype(F32).astype(BF16)
    y_ids = row_ids
    one = jnp.ones((), BF16)
    zero = jnp.zeros((), BF16)
    left = []
    right = []
    for brick in range(SLOTS):
        at = slice(brick, brick + 1)

        def spread(value):
            return jnp.broadcast_to(value[at], (ROWS, LANES)).astype(BF16)

        hit = row_ids == spread(row)
        left.append(
            jnp.concatenate(
                [
                    jnp.where(hit, spread(high), zero),
                    jnp.where(hit, spread(low), zero),
                    jnp.where(hit, one, zero),
                ],
                axis=0,
            )
        )
        right.append(jnp.where(y_ids == spread(y), one, zero))
    return dot(
        jnp.concatenate(left, axis=1), jnp.concatenate(right, axis=1), contract=((1,), (1,))
    )


def shift_rows(value, step):
    zeros = jnp.zeros((abs(step), value.shape[1]), value.dtype)
    if step > 0:
        return jnp.concatenate([value[step:], zeros], axis=0)
    return jnp.concatenate([zeros, value[:step]], axis=0)


def look_chunk(table_high, table_low, code):
    whole = code.astype(jnp.int32)
    row = ((whole // 256) - 1).astype(F32)
    y = (whole % 256).astype(F32)
    y_ids = iota((NY, LANES), 0).astype(F32).astype(BF16)
    row_ids = iota((ROWS, LANES), 0).astype(F32)
    one = jnp.ones((), BF16)
    zero = jnp.zeros((), BF16)
    right = []
    for brick in range(SLOTS):
        spread = jnp.broadcast_to(y[brick : brick + 1], (NY, LANES)).astype(BF16)
        right.append(jnp.where(y_ids == spread, one, zero))
    hot = jnp.concatenate(right, axis=1)
    picked = dot(table_high, hot) + dot(table_low, hot)
    out = []
    for brick in range(SLOTS):
        part = picked[:, brick * LANES : (brick + 1) * LANES]
        hit = row_ids == jnp.broadcast_to(row[brick : brick + 1], (ROWS, LANES))
        out.append(jnp.sum(jnp.where(hit, part, 0.0), axis=0, keepdims=True))
    return jnp.concatenate(out, axis=0)


SIDE = 4
MESH = pl.DeviceIdType.MESH


def prepare(velocity, plane, column, count, send, slot, me):
    used = used_mask(count[...])
    speed = velocity[...]
    kinetic = 0.5 * (speed[0] * speed[0] + speed[1] * speed[1] + speed[2] * speed[2])
    kinetic = jnp.where(used, kinetic, 0.0)
    planes = plane[...]
    columns = column[...]
    owner = planes[:, 0:1] // PLANES
    place = (owner // SIDE - me // SIDE + SIDE) % SIDE * SIDE + (owner % SIDE - me % SIDE + SIDE) % SIDE
    square = (BRICKS, LANES)
    hits = jnp.where(iota(square, 1) == place, 1.0, 0.0)
    earlier = jnp.where(iota(square, 0) > iota(square, 1), 1.0, 0.0).astype(BF16)
    before = dot(earlier, hits.astype(BF16))
    rank = jnp.sum(before * hits, axis=1, keepdims=True)
    brick_slot = place.astype(F32) * SLOTS + rank
    slot[...] = jnp.broadcast_to(brick_slot, square)
    slot_row = jnp.sum(
        jnp.where(iota(square, 0) == iota(square, 1), brick_slot, 0.0), axis=0, keepdims=True
    )
    slots = SLABS * SLOTS
    pick = jnp.where(iota((slots, BRICKS), 0).astype(F32) == slot_row, 1.0, 0.0).astype(BF16)
    row_code = (planes - owner * PLANES) * WIDTH + columns // NY + 1
    row_code = jnp.where(used, row_code, 0).astype(F32).astype(BF16)
    y_code = jnp.where(used, columns % NY, 0).astype(F32).astype(BF16)
    code = 256.0 * dot(pick, row_code) + dot(pick, y_code)
    high, middle, low = split3(kinetic)
    sent = (dot(pick, high) + dot(pick, middle)) + dot(pick, low)
    send[:, 0] = sent.reshape(SLABS, SLOTS, LANES)
    send[:, 1] = code.reshape(SLABS, SLOTS, LANES)


def eliminate(temp, below, left, right, slab, totals, reduced, fixed, to_low, to_high):
    has_below = jnp.where(slab > 0, 1.0, 0.0)
    shape = (WIDTH, NY)
    lower = has_below * (STIFFNESS * (0.5 * (temp[0] + below[...])))
    ground = current = link = back_ground = back_current = None
    for p in range(PLANES):
        here = temp[p]
        energy = totals[p * WIDTH : (p + 1) * WIDTH] + totals[ROWS + p * WIDTH : ROWS + (p + 1) * WIDTH]
        count = totals[2 * ROWS + p * WIDTH : 2 * ROWS + (p + 1) * WIDTH]
        x_less = jnp.concatenate([left[p : p + 1], here[:-1]], axis=0)
        x_more = jnp.concatenate([here[1:], right[p : p + 1]], axis=0)
        y_less = pltpu.roll(here, 1, 1)
        y_more = pltpu.roll(here, NY - 1, 1)
        lateral = LATERAL * (x_less + x_more + y_less + y_more - 4.0 * here)
        excess = here + COUPLE * count
        source = here * here + lateral + (COUPLE * TWO_THIRDS) * energy
        if p == 0:
            link, ground, current = lower, excess, source
            back_ground = back_current = jnp.zeros(shape, F32)
        else:
            upper = STIFFNESS * (0.5 * (temp[p - 1] + here))
            inverse = 1.0 / (ground + link + upper)
            high = upper * inverse
            low = link * inverse
            fixed[p - 1] = current * inverse
            to_low[p - 1] = low
            to_high[p - 1] = high
            back_ground = back_ground + low * ground
            back_current = back_current + low * current
            link = high * link
            ground = excess + high * ground
            current = source + high * current
    for place, value in enumerate([link, ground, current, back_ground, back_current]):
        reduced[:, place, :] = value


def solve_reduced(systems, ends):
    link, ground, current, back_ground, back_current = [systems[:, place, :] for place in range(5)]
    ground = ground + shift_rows(back_ground, 1)
    current = current + shift_rows(back_current, 1)
    below = link
    above = shift_rows(link, 1)
    distance = 1
    while distance < SLABS:
        inverse = 1.0 / (ground + below + above)
        ratio_below = below * shift_rows(inverse, -distance)
        ratio_above = above * shift_rows(inverse, distance)
        ground, current, below, above = (
            ground
            + ratio_below * shift_rows(ground, -distance)
            + ratio_above * shift_rows(ground, distance),
            current
            + ratio_below * shift_rows(current, -distance)
            + ratio_above * shift_rows(current, distance),
            ratio_below * shift_rows(below, -distance),
            ratio_above * shift_rows(above, distance),
        )
        distance *= 2
    value = current / ground
    ends[:, 0, :] = shift_rows(value, -1)
    ends[:, 1, :] = value


def substitute(fixed, to_low, to_high, ends, solved, high_table, low_table):
    low_end = ends[:, 0, :]
    value = ends[:, 1, :]
    for p in range(PLANES - 1, -1, -1):
        if p < PLANES - 1:
            value = (fixed[p] + to_low[p] * low_end) + to_high[p] * value
        solved[p] = value
        high, low = split2(value)
        high_table[p * WIDTH : (p + 1) * WIDTH] = high
        low_table[p * WIDTH : (p + 1) * WIDTH] = low


def kick(velocity, noise, count, slot, returned, moved):
    used = used_mask(count[...])
    slots = SLABS * SLOTS
    slot_ids = iota((BRICKS, slots), 1).astype(F32)
    where_from = jnp.concatenate([slot[...], slot[...]], axis=1)
    pick = jnp.where(slot_ids == where_from, 1.0, 0.0).astype(BF16)
    high, middle, low = split3(returned[...].reshape(slots, LANES))
    temp = (dot(pick, high) + dot(pick, middle)) + dot(pick, low)
    scale = jnp.sqrt(2.0 * KICK_RATE * temp)
    for axis in range(3):
        kicked = (1.0 - KICK_RATE) * velocity[axis] + scale * noise[axis]
        moved[axis] = jnp.where(used, kicked, 0.0)


def step_kernel(
    velocity_in, noise_in, plane_in, column_in, count_in, temp_in,
    solved_out, moved_out,
    velocity, noise, plane, column, count, temp,
    send, got, slot, edges, below, sides, totals, reduced, systems, ends, own_ends,
    fixed, to_low, to_high, solved, high_table, low_table, reply, returned, moved,
    load_sem, store_sem, halo_send, halo_recv,
    atom_send, atom_recv, system_send, system_recv, end_send, end_recv, reply_send, reply_recv,
):
    me = lax.axis_index("gz")
    line = lax.axis_index("gx")
    lines = lax.axis_size("gx")
    next_line = lax.rem(line + 1, lines)
    last_line = lax.rem(line + lines - 1, lines)
    deep, wide = me // SIDE, me % SIDE

    def ahead(place):
        return (deep + place // SIDE) % SIDE * SIDE + (wide + place % SIDE) % SIDE

    def behind(place):
        return (deep + SIDE - place // SIDE) % SIDE * SIDE + (wide + SIDE - place % SIDE) % SIDE

    def remote(source, target, sent, received, where):
        return pltpu.make_async_remote_copy(
            src_ref=source, dst_ref=target, send_sem=sent, recv_sem=received,
            device_id=where, device_id_type=MESH,
        )

    loads = [
        pltpu.make_async_copy(source, target, load_sem.at[place])
        for place, (source, target) in enumerate(
            [
                (plane_in, plane),
                (column_in, column),
                (count_in, count),
                (velocity_in, velocity),
                (temp_in, temp),
                (noise_in, noise),
            ]
        )
    ]
    for load in loads:
        load.start()
    barrier = pltpu.get_barrier_semaphore()
    for place in range(1, SLABS):
        pl.semaphore_signal(barrier, inc=1, device_id={"gz": ahead(place)}, device_id_type=MESH)
    for where in (next_line, last_line):
        pl.semaphore_signal(barrier, inc=1, device_id={"gx": where}, device_id_type=MESH)
    for load in loads[:4]:
        load.wait()
    prepare(velocity, plane, column, count, send, slot, me)
    pl.semaphore_wait(barrier, SLABS + 1)

    def atoms(place):
        return remote(
            send.at[place], got.at[place], atom_send.at[place], atom_recv.at[place], {"gz": ahead(place)}
        )

    for place in range(1, SLABS):
        atoms(place).start()
    got[0] = send[0]
    loads[4].wait()
    edges[0] = temp[:, 0, :]
    edges[1] = temp[:, WIDTH - 1, :]
    halos = [
        remote(temp.at[PLANES - 1], below, halo_send.at[0], halo_recv.at[0], {"gz": (me + 1) % SLABS}),
        remote(edges.at[1], sides.at[0], halo_send.at[1], halo_recv.at[1], {"gx": next_line}),
        remote(edges.at[0], sides.at[1], halo_send.at[2], halo_recv.at[2], {"gx": last_line}),
    ]
    for halo in halos:
        halo.start()

    totals[...] = jnp.zeros_like(totals)

    def add_chunk(place, carry):
        @pl.when(place > 0)
        def _():
            atoms(place).wait_recv()

        totals[...] += bin_chunk(got[place, 0], got[place, 1])
        return carry

    lax.fori_loop(0, SLABS, add_chunk, 0)
    for halo in halos:
        halo.wait_recv()
    eliminate(temp, below, sides.at[0], sides.at[1], me, totals, reduced, fixed, to_low, to_high)

    def system(place):
        return remote(
            reduced.at[ahead(place)], systems.at[me], system_send.at[place], system_recv.at[place],
            {"gz": ahead(place)},
        )

    for place in range(1, SLABS):
        system(place).start()
    systems[me] = reduced[me]
    for place in range(1, SLABS):
        system(place).wait_recv()
    solve_reduced(systems, ends)

    def end(place):
        return remote(
            ends.at[ahead(place)], own_ends.at[me], end_send.at[place], end_recv.at[place],
            {"gz": ahead(place)},
        )

    for place in range(1, SLABS):
        end(place).start()
    own_ends[me] = ends[me]
    for place in range(1, SLABS):
        end(place).wait_recv()
    substitute(fixed, to_low, to_high, own_ends, solved, high_table, low_table)
    keep = pltpu.make_async_copy(solved, solved_out, store_sem.at[0])
    keep.start()

    def answer(place):
        return remote(
            reply.at[place], returned.at[place], reply_send.at[place], reply_recv.at[place],
            {"gz": behind(place)},
        )

    def look(turn, carry):
        place = SLABS - 1 - turn
        reply[place] = look_chunk(high_table[...], low_table[...], got[place, 1])

        @pl.when(place > 0)
        def _():
            answer(place).start()

        return carry

    lax.fori_loop(0, SLABS, look, 0)
    returned[0] = reply[0]
    loads[5].wait()
    for place in range(1, SLABS):
        answer(place).wait_recv()
    kick(velocity, noise, count, slot, returned, moved)
    leave = pltpu.make_async_copy(moved, moved_out, store_sem.at[1])
    leave.start()
    for halo in halos:
        halo.wait_send()
    for place in range(1, SLABS):
        atoms(place).wait_send()
        system(place).wait_send()
        end(place).wait_send()
        answer(place).wait_send()
    keep.wait()
    leave.wait()


def shape(*dims):
    return jax.ShapeDtypeStruct(dims, F32)


def body(velocity, noise, plane, column, brick_count, temp):
    count = brick_count.reshape(1, BRICKS)
    vmem = pltpu.VMEM
    inner = vmem((PLANES - 1, WIDTH, NY), F32)
    chunk = vmem((SLABS, 2, SLOTS, LANES), F32)
    line = vmem((SLABS, SLOTS, LANES), F32)
    table = vmem((ROWS, NY), BF16)
    pairs = pltpu.SemaphoreType.DMA((SLABS,))
    return pl.pallas_call(
        step_kernel,
        out_shape=(shape(PLANES, WIDTH, NY), shape(3, BRICKS, LANES)),
        in_specs=[pl.BlockSpec(memory_space=pl.ANY)] * 6,
        out_specs=(pl.BlockSpec(memory_space=pl.ANY),) * 2,
        scratch_shapes=[
            vmem((3, BRICKS, LANES), F32),
            vmem((3, BRICKS, LANES), F32),
            vmem((BRICKS, LANES), jnp.int32),
            vmem((BRICKS, LANES), jnp.int32),
            vmem((1, BRICKS), jnp.int32),
            vmem((PLANES, WIDTH, NY), F32),
            chunk,
            chunk,
            vmem((BRICKS, LANES), F32),
            vmem((2, PLANES, NY), F32),
            vmem((WIDTH, NY), F32),
            vmem((2, PLANES, NY), F32),
            vmem((3 * ROWS, NY), F32),
            vmem((WIDTH, 5, NY), F32),
            vmem((SLABS, 5, NY), F32),
            vmem((SLABS, 2, NY), F32),
            vmem((WIDTH, 2, NY), F32),
            inner,
            inner,
            inner,
            vmem((PLANES, WIDTH, NY), F32),
            table,
            table,
            line,
            line,
            vmem((3, BRICKS, LANES), F32),
            pltpu.SemaphoreType.DMA((6,)),
            pltpu.SemaphoreType.DMA((2,)),
            pltpu.SemaphoreType.DMA((3,)),
            pltpu.SemaphoreType.DMA((3,)),
        ]
        + [pairs] * 8,
        compiler_params=pltpu.CompilerParams(collective_id=0, has_side_effects=True),
    )(velocity, noise, plane, column, count, temp)


def solution(mesh):
    placed = (
        P(None, ("gz", "gx"), None),
        P(None, ("gz", "gx"), None),
        P(("gz", "gx"), None),
        P(("gz", "gx"), None),
        P(("gz", "gx")),
        P("gz", "gx", None),
    )
    return jax.shard_map(
        body,
        mesh=mesh,
        in_specs=placed,
        out_specs=(P("gz", "gx", None), P(None, ("gz", "gx"), None)),
        check_vma=False,
    )
```

time: 99 us -> 54.5 us (0.55)
  blocking collectives: 38.4 us -> 0 us
  starting transfers between devices: 13.4 us -> 0 us
  Pallas kernels: 38.5 us -> 51.3 us
  waiting for transfers between devices: 4.37 us -> 0 us
    all_to_all x3 -> x0, blocking collectives: 38.4 us -> none  [the longest x1 14.6 us: body(): systems = lax.all_to_all(reduced, 'gz', 0, 0, tiled=True)]
    pallas_call x5 -> x1, Pallas kernels: 38.5 us -> 51.3 us  [body(): pl.pallas_call(step_kernel, out_shape=(shape(PLANES, WIDTH, NY), shape(3,...]
    all_to_all x1 -> x0, starting transfers between devices: 7.99 us -> none  [body(): got = lax.all_to_all(send, 'gz', 0, 0, tiled=True)]
    ppermute x3 -> x0, starting transfers between devices: 5.44 us -> none  [ring(): return lax.ppermute(value, axis, pairs)]
    ppermute x3 -> x0, waiting for transfers between devices: 4.36 us -> none  [ring(): return lax.ppermute(value, axis, pairs)]
    slice x2 -> x0, local copies, waits for them, and re-layouts: 1.72 us -> none  [the longest x1 0.99 us: body(): right = ring(temp[:, :1], 'gx', -1, True)]
    unnamed x8 -> x4, local copies, waits for them, and re-layouts: 1.3 us -> 2.39 us
  transfers between devices with their start and end apart: 4 -> 0, of which waited for: 2 -> 0; matrix products, arithmetic and copies ran while one was open for 2% -> 0% of each run, Pallas kernels for 0% -> 0%
where the time goes in v1:
time: 54.5 us; the launch traced here: 54.3 us
  Pallas kernels  51.3 us (94%)
  local copies, waits for them, and re-layouts  2.39 us (4%)
  between operations  0.65 us (1%)
    pallas_call x1, Pallas kernels, body(): pl.pallas_call(step_kernel, out_shape=(shape(PLANES, WIDTH, NY), shape(3,...  51.3 us
    unnamed x4, local copies, waits for them, and re-layouts  2.39 us

profile of v1, /device:TPU:0, one launch (start us, length us, event | category | flops | bytes accessed | tf_op | source)
XLA Modules:
  0.0 54.3 jit_solution(12800148169055312858)
XLA Ops:
  0.6 51.3 %shard_map.77 = (f32[16,16,256]{2,1,0:T(8,128)}, f32[3,128,128]{2,1,0:T(8,128)}) custom-call(f32[3,128,128]{2,1,0:T(8,128)} %velocity_in.1, f32[3,128,128]{2,1,0:T(8,128)} %noise_in.1, s32[128,128]{1,0:T(8,128)} %plane_in.1, s32[128,128]{1,0:T(8,128)} %column_in.1, s32[1,128]{1,0:T(1,128)} %bitcast.1, f32[16,16,256]{2,1,0:T(8,128)} %temp_in.1), custom_call_target="tpu_custom_call" | custom-call | tf_op jit(solution)/shard_map/pallas_call | solution.py:406
  51.9 0.0 copy-start
  51.9 1.7 %copy.10 = f32[16,16,256]{2,1,0:T(8,128)} copy(f32[16,16,256]{2,1,0:T(8,128)} %get-tuple-element.4) | data formatting | bytes 524288
  53.7 0.0 copy-done
  53.7 0.7 %copy.11 = f32[3,128,128]{2,1,0:T(8,128)} copy(f32[3,128,128]{2,1,0:T(8,128)S(1)} %copy-done) | data formatting | bytes 393216
Async XLA Ops:
  51.9 1.7 %copy-start = (f32[3,128,128]{2,1,0:T(8,128)S(1)}, f32[3,128,128]{2,1,0:T(8,128)}, u32[]{:S(2)}) copy-start(f32[3,128,128]{2,1,0:T(8,128)} %get-tuple-element.5) | copy-start | bytes 589828

commit v2 on v1

--- a/solution.py
+++ b/solution.py
@@ -53,39 +53,70 @@
 ROWS = PLANES * WIDTH
 
 
+HALF = ROWS // 2
+LOW_WEIGHT, HIGH_WEIGHT = 1.0 / 16.0, 256.0
+
+
+def decode(code):
+    whole = code.astype(jnp.int32)
+    return whole // 256 - 1, whole % 256
+
+
+def constant(value):
+    return jnp.full((), value, BF16)
+
+
 def bin_chunk(kinetic, code):
-    whole = code.astype(jnp.int32)
-    row = ((whole // 256) - 1).astype(F32)
-    y = (whole % 256).astype(F32)
+    row, y = decode(code)
+    row, y = row.astype(F32), y.astype(F32)
     high = kinetic.astype(BF16).astype(F32)
     low = kinetic - high
-    row_ids = iota((ROWS, LANES), 0).astype(F32).astype(BF16)
-    y_ids = row_ids
-    one = jnp.ones((), BF16)
-    zero = jnp.zeros((), BF16)
+    ids = iota((ROWS, LANES), 0).astype(F32).astype(BF16)
+    zero = constant(0.0)
     left = []
     right = []
     for brick in range(SLOTS):
-        at = slice(brick, brick + 1)
 
         def spread(value):
-            return jnp.broadcast_to(value[at], (ROWS, LANES)).astype(BF16)
-
-        hit = row_ids == spread(row)
+            return jnp.broadcast_to(value[brick : brick + 1], (ROWS, LANES)).astype(BF16)
+
+        hit = ids == spread(row)
+        second = jnp.where(hit[HALF:], constant(HIGH_WEIGHT), zero)
         left.append(
             jnp.concatenate(
                 [
                     jnp.where(hit, spread(high), zero),
                     jnp.where(hit, spread(low), zero),
-                    jnp.where(hit, one, zero),
+                    jnp.where(hit[:HALF], constant(LOW_WEIGHT), second),
                 ],
                 axis=0,
             )
         )
-        right.append(jnp.where(y_ids == spread(y), one, zero))
+        right.append(jnp.where(ids == spread(y), constant(1.0), zero))
     return dot(
         jnp.concatenate(left, axis=1), jnp.concatenate(right, axis=1), contract=((1,), (1,))
     )
+
+
+def add_up(values):
+    while len(values) > 1:
+        values = [sum(values[i : i + 2]) for i in range(0, len(values), 2)]
+    return values[0]
+
+
+def bin_group(chunks, energy, counts, first):
+    parts = [bin_chunk(kinetic, code) for kinetic, code in chunks]
+    packed = [part[2 * ROWS :] for part in parts]
+    upper = [jnp.floor(part * (1.0 / HIGH_WEIGHT)) for part in packed]
+    lower = [part - HIGH_WEIGHT * more for part, more in zip(packed, upper)]
+    sums = [
+        add_up([part[:ROWS] + part[ROWS : 2 * ROWS] for part in parts]),
+        add_up(lower) * (1.0 / LOW_WEIGHT),
+        add_up(upper),
+    ]
+    places = [(energy, slice(None)), (counts, slice(0, HALF)), (counts, slice(HALF, ROWS))]
+    for (target, rows), value in zip(places, sums):
+        target[rows] = value if first else target[rows] + value
 
 
 def shift_rows(value, step):
@@ -95,20 +126,17 @@
     return jnp.concatenate([zeros, value[:step]], axis=0)
 
 
-def look_chunk(table_high, table_low, code):
-    whole = code.astype(jnp.int32)
-    row = ((whole // 256) - 1).astype(F32)
-    y = (whole % 256).astype(F32)
+def look_chunk(high_table, low_table, code):
+    row, y = decode(code)
+    row, y = row.astype(F32), y.astype(F32)
     y_ids = iota((NY, LANES), 0).astype(F32).astype(BF16)
     row_ids = iota((ROWS, LANES), 0).astype(F32)
-    one = jnp.ones((), BF16)
-    zero = jnp.zeros((), BF16)
     right = []
     for brick in range(SLOTS):
         spread = jnp.broadcast_to(y[brick : brick + 1], (NY, LANES)).astype(BF16)
-        right.append(jnp.where(y_ids == spread, one, zero))
+        right.append(jnp.where(y_ids == spread, constant(1.0), constant(0.0)))
     hot = jnp.concatenate(right, axis=1)
-    picked = dot(table_high, hot) + dot(table_low, hot)
+    picked = dot(high_table, hot) + dot(low_table, hot)
     out = []
     for brick in range(SLOTS):
         part = picked[:, brick * LANES : (brick + 1) * LANES]
@@ -152,15 +180,15 @@
     send[:, 1] = code.reshape(SLABS, SLOTS, LANES)
 
 
-def eliminate(temp, below, left, right, slab, totals, reduced, fixed, to_low, to_high):
+def eliminate(temp, below, left, right, slab, energies, counts, reduced, fixed, to_low, to_high):
     has_below = jnp.where(slab > 0, 1.0, 0.0)
     shape = (WIDTH, NY)
     lower = has_below * (STIFFNESS * (0.5 * (temp[0] + below[...])))
     ground = current = link = back_ground = back_current = None
     for p in range(PLANES):
         here = temp[p]
-        energy = totals[p * WIDTH : (p + 1) * WIDTH] + totals[ROWS + p * WIDTH : ROWS + (p + 1) * WIDTH]
-        count = totals[2 * ROWS + p * WIDTH : 2 * ROWS + (p + 1) * WIDTH]
+        energy = energies[p * WIDTH : (p + 1) * WIDTH]
+        count = counts[p * WIDTH : (p + 1) * WIDTH]
         x_less = jnp.concatenate([left[p : p + 1], here[:-1]], axis=0)
         x_more = jnp.concatenate([here[1:], right[p : p + 1]], axis=0)
         y_less = pltpu.roll(here, 1, 1)
@@ -243,11 +271,11 @@
 
 def step_kernel(
     velocity_in, noise_in, plane_in, column_in, count_in, temp_in,
-    solved_out, moved_out,
+    solved, moved,
     velocity, noise, plane, column, count, temp,
-    send, got, slot, edges, below, sides, totals, reduced, systems, ends, own_ends,
-    fixed, to_low, to_high, solved, high_table, low_table, reply, returned, moved,
-    load_sem, store_sem, halo_send, halo_recv,
+    send, got, slot, edges, below, sides, energies, counts, reduced, systems, ends, own_ends,
+    fixed, to_low, to_high, high_table, low_table, reply, returned,
+    load_sem, halo_send, halo_recv,
     atom_send, atom_recv, system_send, system_recv, end_send, end_recv, reply_send, reply_recv,
 ):
     me = lax.axis_index("gz")
@@ -292,6 +320,7 @@
     for load in loads[:4]:
         load.wait()
     prepare(velocity, plane, column, count, send, slot, me)
+    bin_group([(send[0, 0], send[0, 1])], energies, counts, True)
     pl.semaphore_wait(barrier, SLABS + 1)
 
     def atoms(place):
@@ -301,7 +330,6 @@
 
     for place in range(1, SLABS):
         atoms(place).start()
-    got[0] = send[0]
     loads[4].wait()
     edges[0] = temp[:, 0, :]
     edges[1] = temp[:, WIDTH - 1, :]
@@ -313,20 +341,21 @@
     for halo in halos:
         halo.start()
 
-    totals[...] = jnp.zeros_like(totals)
-
-    def add_chunk(place, carry):
-        @pl.when(place > 0)
-        def _():
+    def bin_places(places):
+        for place in places:
             atoms(place).wait_recv()
-
-        totals[...] += bin_chunk(got[place, 0], got[place, 1])
+        bin_group([(got[place, 0], got[place, 1]) for place in places], energies, counts, False)
+
+    bin_places(range(1, SIDE))
+
+    def bin_turn(turn, carry):
+        bin_places([turn * SIDE + i for i in range(SIDE)])
         return carry
 
-    lax.fori_loop(0, SLABS, add_chunk, 0)
+    lax.fori_loop(1, SIDE, bin_turn, 0)
     for halo in halos:
         halo.wait_recv()
-    eliminate(temp, below, sides.at[0], sides.at[1], me, totals, reduced, fixed, to_low, to_high)
+    eliminate(temp, below, sides.at[0], sides.at[1], me, energies, counts, reduced, fixed, to_low, to_high)
 
     def system(place):
         return remote(
@@ -353,8 +382,6 @@
     for place in range(1, SLABS):
         end(place).wait_recv()
     substitute(fixed, to_low, to_high, own_ends, solved, high_table, low_table)
-    keep = pltpu.make_async_copy(solved, solved_out, store_sem.at[0])
-    keep.start()
 
     def answer(place):
         return remote(
@@ -362,24 +389,29 @@
             {"gz": behind(place)},
         )
 
-    def look(turn, carry):
-        place = SLABS - 1 - turn
-        reply[place] = look_chunk(high_table[...], low_table[...], got[place, 1])
-
-        @pl.when(place > 0)
-        def _():
+    def look_places(places, target):
+        values = [
+            look_chunk(high_table[...], low_table[...], source[place, 1]) for source, place in places
+        ]
+        for (_, place), value in zip(places, values):
+            target[place] = value
+
+    def look_turn(turn, carry):
+        places = [(SIDE - 1 - turn) * SIDE + i for i in range(SIDE)]
+        look_places([(got, place) for place in places], reply)
+        for place in places:
             answer(place).start()
-
         return carry
 
-    lax.fori_loop(0, SLABS, look, 0)
-    returned[0] = reply[0]
+    lax.fori_loop(0, SIDE - 1, look_turn, 0)
+    look_places([(got, place) for place in range(1, SIDE)], reply)
+    for place in range(1, SIDE):
+        answer(place).start()
+    look_places([(send, 0)], returned)
     loads[5].wait()
     for place in range(1, SLABS):
         answer(place).wait_recv()
     kick(velocity, noise, count, slot, returned, moved)
-    leave = pltpu.make_async_copy(moved, moved_out, store_sem.at[1])
-    leave.start()
     for halo in halos:
         halo.wait_send()
     for place in range(1, SLABS):
@@ -387,8 +419,17 @@
         system(place).wait_send()
         end(place).wait_send()
         answer(place).wait_send()
-    keep.wait()
-    leave.wait()
+
+
+def store_kernel(solved, moved, solved_out, moved_out, sems):
+    copies = [
+        pltpu.make_async_copy(solved, solved_out, sems.at[0]),
+        pltpu.make_async_copy(moved, moved_out, sems.at[1]),
+    ]
+    for copy in copies:
+        copy.start()
+    for copy in copies:
+        copy.wait()
 
 
 def shape(*dims):
@@ -403,11 +444,12 @@
     line = vmem((SLABS, SLOTS, LANES), F32)
     table = vmem((ROWS, NY), BF16)
     pairs = pltpu.SemaphoreType.DMA((SLABS,))
-    return pl.pallas_call(
+    outs = (shape(PLANES, WIDTH, NY), shape(3, BRICKS, LANES))
+    solved, moved = pl.pallas_call(
         step_kernel,
-        out_shape=(shape(PLANES, WIDTH, NY), shape(3, BRICKS, LANES)),
+        out_shape=(vmem((PLANES, WIDTH, NY), F32), vmem((3, BRICKS, LANES), F32)),
         in_specs=[pl.BlockSpec(memory_space=pl.ANY)] * 6,
-        out_specs=(pl.BlockSpec(memory_space=pl.ANY),) * 2,
+        out_specs=(pl.BlockSpec(memory_space=pltpu.VMEM),) * 2,
         scratch_shapes=[
             vmem((3, BRICKS, LANES), F32),
             vmem((3, BRICKS, LANES), F32),
@@ -421,7 +463,8 @@
             vmem((2, PLANES, NY), F32),
             vmem((WIDTH, NY), F32),
             vmem((2, PLANES, NY), F32),
-            vmem((3 * ROWS, NY), F32),
+            vmem((ROWS, NY), F32),
+            vmem((ROWS, NY), F32),
             vmem((WIDTH, 5, NY), F32),
             vmem((SLABS, 5, NY), F32),
             vmem((SLABS, 2, NY), F32),
@@ -429,20 +472,24 @@
             inner,
             inner,
             inner,
-            vmem((PLANES, WIDTH, NY), F32),
             table,
             table,
             line,
             line,
-            vmem((3, BRICKS, LANES), F32),
             pltpu.SemaphoreType.DMA((6,)),
-            pltpu.SemaphoreType.DMA((2,)),
             pltpu.SemaphoreType.DMA((3,)),
             pltpu.SemaphoreType.DMA((3,)),
         ]
         + [pairs] * 8,
         compiler_params=pltpu.CompilerParams(collective_id=0, has_side_effects=True),
     )(velocity, noise, plane, column, count, temp)
+    return pl.pallas_call(
+        store_kernel,
+        out_shape=outs,
+        in_specs=[pl.BlockSpec(memory_space=pltpu.VMEM)] * 2,
+        out_specs=(pl.BlockSpec(memory_space=pl.ANY),) * 2,
+        scratch_shapes=[pltpu.SemaphoreType.DMA((2,))],
+    )(*[pltpu.with_memory_space_constraint(value, pltpu.VMEM) for value in (solved, moved)])
 
 
 def solution(mesh):

time: 54.5 us -> 48.5 us (0.89)
  Pallas kernels: 51.3 us -> 47.7 us
  local copies, waits for them, and re-layouts: 2.39 us -> 0 us
    pallas_call x1 -> x2, Pallas kernels: 51.3 us -> 47.7 us  [the longest x1 47 us: body(): pl.pallas_call(step_kernel, out_shape=(vmem((PLANES, WIDTH, NY), F32), vm...]
    unnamed x4 -> x0, local copies, waits for them, and re-layouts: 2.39 us -> none
where the time goes in v2:
time: 48.5 us; the launch traced here: 48.4 us
  Pallas kernels  47.7 us (98%)
  between operations  0.64 us (1%)
    pallas_call x1, Pallas kernels, body(): pl.pallas_call(step_kernel, out_shape=(vmem((PLANES, WIDTH, NY), F32), vm...  47 us

profile of v2, /device:TPU:0, one launch (start us, length us, event | category | flops | bytes accessed | tf_op | source)
XLA Modules:
  0.0 48.4 jit_solution(4530877433204836991)
XLA Ops:
  0.6 47.0 %shard_map.77 = (f32[16,16,256]{2,1,0:T(8,128)S(1)}, f32[3,128,128]{2,1,0:T(8,128)S(1)}) custom-call(f32[3,128,128]{2,1,0:T(8,128)} %velocity_in.1, f32[3,128,128]{2,1,0:T(8,128)} %noise_in.1, s32[128,128]{1,0:T(8,128)} %plane_in.1, s32[128,128]{1,0:T(8,128)} %column_in.1, s32[1,128]{1,0:T(1,128)} %bitcast.1, f32[16,16,256]{2,1,0:T(8,128)} %temp_in.1), custom_call_target="tpu_custom_call" | custom-call | tf_op jit(solution)/shard_map/pallas_call | solution.py:448
  47.6 0.8 %shard_map.78 = (f32[16,16,256]{2,1,0:T(8,128)}, f32[3,128,128]{2,1,0:T(8,128)}) custom-call(f32[16,16,256]{2,1,0:T(8,128)S(1)} %get-tuple-element.4.solved, f32[3,128,128]{2,1,0:T(8,128)S(1)} %get-tuple-element.5.moved), custom_call_target="tpu_custom_call" | custom-call | tf_op jit(solution)/shard_map/pallas_call | solution.py:486

commit v3 on v2

--- a/solution.py
+++ b/solution.py
@@ -53,8 +53,8 @@
 ROWS = PLANES * WIDTH
 
 
-HALF = ROWS // 2
-LOW_WEIGHT, HIGH_WEIGHT = 1.0 / 16.0, 256.0
+F8 = jnp.float8_e4m3fn
+LOW_SCALE = 4096.0
 
 
 def decode(code):
@@ -70,32 +70,32 @@
     row, y = decode(code)
     row, y = row.astype(F32), y.astype(F32)
     high = kinetic.astype(BF16).astype(F32)
-    low = kinetic - high
+    low = (kinetic - high) * LOW_SCALE
     ids = iota((ROWS, LANES), 0).astype(F32).astype(BF16)
-    zero = constant(0.0)
-    left = []
-    right = []
+    one, zero = constant(1.0), constant(0.0)
+    left, left_low, right = [], [], []
     for brick in range(SLOTS):
 
         def spread(value):
             return jnp.broadcast_to(value[brick : brick + 1], (ROWS, LANES)).astype(BF16)
 
         hit = ids == spread(row)
-        second = jnp.where(hit[HALF:], constant(HIGH_WEIGHT), zero)
-        left.append(
+        left.append(jnp.where(hit, spread(high), zero))
+        left_low.append(
             jnp.concatenate(
                 [
-                    jnp.where(hit, spread(high), zero),
-                    jnp.where(hit, spread(low), zero),
-                    jnp.where(hit[:HALF], constant(LOW_WEIGHT), second),
+                    jnp.where(hit, spread(low), zero).astype(F8),
+                    jnp.where(hit, one, zero).astype(F8),
                 ],
                 axis=0,
             )
         )
-        right.append(jnp.where(ids == spread(y), constant(1.0), zero))
-    return dot(
-        jnp.concatenate(left, axis=1), jnp.concatenate(right, axis=1), contract=((1,), (1,))
-    )
+        right.append(jnp.where(ids == spread(y), one, zero))
+    last = ((1,), (1,))
+    upper = dot(jnp.concatenate(left, axis=1), jnp.concatenate(right, axis=1), contract=last)
+    right_low = jnp.concatenate([value.astype(F8) for value in right], axis=1)
+    rest = dot(jnp.concatenate(left_low, axis=1), right_low, contract=last)
+    return upper + rest[:ROWS] * (1.0 / LOW_SCALE), rest[ROWS:]
 
 
 def add_up(values):
@@ -106,17 +106,9 @@
 
 def bin_group(chunks, energy, counts, first):
     parts = [bin_chunk(kinetic, code) for kinetic, code in chunks]
-    packed = [part[2 * ROWS :] for part in parts]
-    upper = [jnp.floor(part * (1.0 / HIGH_WEIGHT)) for part in packed]
-    lower = [part - HIGH_WEIGHT * more for part, more in zip(packed, upper)]
-    sums = [
-        add_up([part[:ROWS] + part[ROWS : 2 * ROWS] for part in parts]),
-        add_up(lower) * (1.0 / LOW_WEIGHT),
-        add_up(upper),
-    ]
-    places = [(energy, slice(None)), (counts, slice(0, HALF)), (counts, slice(HALF, ROWS))]
-    for (target, rows), value in zip(places, sums):
-        target[rows] = value if first else target[rows] + value
+    for target, values in zip((energy, counts), zip(*parts)):
+        value = add_up(list(values))
+        target[...] = value if first else target[...] + value
 
 
 def shift_rows(value, step):
@@ -126,27 +118,60 @@
     return jnp.concatenate([zeros, value[:step]], axis=0)
 
 
-def look_chunk(high_table, low_table, code):
+BAND = 8
+
+
+def bit_of(value, bit):
+    return ((value >> bit) & 1) == 1
+
+
+def look_product(high_table, low_table, code):
     row, y = decode(code)
-    row, y = row.astype(F32), y.astype(F32)
+    y = y.astype(F32)
     y_ids = iota((NY, LANES), 0).astype(F32).astype(BF16)
-    row_ids = iota((ROWS, LANES), 0).astype(F32)
     right = []
-    for brick in range(SLOTS):
+    for brick in range(BAND):
         spread = jnp.broadcast_to(y[brick : brick + 1], (NY, LANES)).astype(BF16)
         right.append(jnp.where(y_ids == spread, constant(1.0), constant(0.0)))
     hot = jnp.concatenate(right, axis=1)
     picked = dot(high_table, hot) + dot(low_table, hot)
     out = []
-    for brick in range(SLOTS):
-        part = picked[:, brick * LANES : (brick + 1) * LANES]
-        hit = row_ids == jnp.broadcast_to(row[brick : brick + 1], (ROWS, LANES))
-        out.append(jnp.sum(jnp.where(hit, part, 0.0), axis=0, keepdims=True))
+    for brick in range(BAND):
+        part = picked[:, brick * LANES : (brick + 1) * LANES].reshape(ROWS // 8, 8, LANES)
+        mine = jnp.broadcast_to(row[brick : brick + 1], (8, LANES))
+        for bit in (7, 6, 5, 4, 3):
+            half = part.shape[0] // 2
+            part = jnp.where(bit_of(mine, bit)[None], part[half:], part[:half])
+        hit = iota((8, LANES), 0) == (mine & 7)
+        out.append(jnp.sum(jnp.where(hit, part[0], 0.0), axis=0, keepdims=True))
     return jnp.concatenate(out, axis=0)
+
+
+def look_lanes(table, code):
+    row, y = decode(code)
+    lane, second = y % LANES, y >= LANES
+
+    def pick(values):
+        return jnp.take_along_axis(jnp.broadcast_to(values, (BAND, LANES)), lane, axis=1)
+
+    def tree(start, size):
+        if size == 1:
+            values = table[start // WIDTH, start % WIDTH : start % WIDTH + 1, :]
+            return jnp.where(second, pick(values[:, LANES:]), pick(values[:, :LANES]))
+        half = size // 2
+        return jnp.where(
+            bit_of(row, half.bit_length() - 1), tree(start + half, half), tree(start, half)
+        )
+
+    return tree(0, ROWS)
 
 
 SIDE = 4
 MESH = pl.DeviceIdType.MESH
+WIDE_PEERS = [1, 2, 3]
+DEEP_PEERS = [SIDE, 2 * SIDE, 3 * SIDE]
+HOPS = [0, 1, 2, 1]
+FAR_FIRST = sorted(range(1, SLABS), key=lambda p: -(HOPS[p // SIDE] + HOPS[p % SIDE]))
 
 
 def prepare(velocity, plane, column, count, send, slot, me):
@@ -275,7 +300,7 @@
     velocity, noise, plane, column, count, temp,
     send, got, slot, edges, below, sides, energies, counts, reduced, systems, ends, own_ends,
     fixed, to_low, to_high, high_table, low_table, reply, returned,
-    load_sem, halo_send, halo_recv,
+    row_ready, load_sem, halo_send, halo_recv,
     atom_send, atom_recv, system_send, system_recv, end_send, end_recv, reply_send, reply_recv,
 ):
     me = lax.axis_index("gz")
@@ -313,7 +338,7 @@
     for load in loads:
         load.start()
     barrier = pltpu.get_barrier_semaphore()
-    for place in range(1, SLABS):
+    for place in WIDE_PEERS + DEEP_PEERS:
         pl.semaphore_signal(barrier, inc=1, device_id={"gz": ahead(place)}, device_id_type=MESH)
     for where in (next_line, last_line):
         pl.semaphore_signal(barrier, inc=1, device_id={"gx": where}, device_id_type=MESH)
@@ -321,14 +346,16 @@
         load.wait()
     prepare(velocity, plane, column, count, send, slot, me)
     bin_group([(send[0, 0], send[0, 1])], energies, counts, True)
-    pl.semaphore_wait(barrier, SLABS + 1)
+    pl.semaphore_wait(barrier, len(WIDE_PEERS + DEEP_PEERS) + 2)
 
     def atoms(place):
         return remote(
             send.at[place], got.at[place], atom_send.at[place], atom_recv.at[place], {"gz": ahead(place)}
         )
 
-    for place in range(1, SLABS):
+    for place in DEEP_PEERS:
+        pl.semaphore_signal(row_ready, inc=1, device_id={"gz": ahead(place)}, device_id_type=MESH)
+    for place in WIDE_PEERS + DEEP_PEERS:
         atoms(place).start()
     loads[4].wait()
     edges[0] = temp[:, 0, :]
@@ -338,8 +365,13 @@
         remote(edges.at[1], sides.at[0], halo_send.at[1], halo_recv.at[1], {"gx": next_line}),
         remote(edges.at[0], sides.at[1], halo_send.at[2], halo_recv.at[2], {"gx": last_line}),
     ]
-    for halo in halos:
+    for halo in halos[1:]:
         halo.start()
+    pl.semaphore_wait(row_ready, len(DEEP_PEERS))
+    for place in range(SIDE, SLABS):
+        if place % SIDE:
+            atoms(place).start()
+    halos[0].start()
 
     def bin_places(places):
         for place in places:
@@ -363,7 +395,7 @@
             {"gz": ahead(place)},
         )
 
-    for place in range(1, SLABS):
+    for place in FAR_FIRST:
         system(place).start()
     systems[me] = reduced[me]
     for place in range(1, SLABS):
@@ -376,7 +408,7 @@
             {"gz": ahead(place)},
         )
 
-    for place in range(1, SLABS):
+    for place in FAR_FIRST:
         end(place).start()
     own_ends[me] = ends[me]
     for place in range(1, SLABS):
@@ -390,11 +422,16 @@
         )
 
     def look_places(places, target):
-        values = [
-            look_chunk(high_table[...], low_table[...], source[place, 1]) for source, place in places
-        ]
-        for (_, place), value in zip(places, values):
-            target[place] = value
+        bands = [(source, place, band) for source, place in places for band in (0, BAND)]
+        values = []
+        for number, (source, place, band) in enumerate(bands):
+            code = source[place, 1][band : band + BAND]
+            if number * 8 < len(bands) * 5:
+                values.append(look_product(high_table[...], low_table[...], code))
+            else:
+                values.append(look_lanes(solved, code))
+        for (_, place, band), value in zip(bands, values):
+            target[place, band : band + BAND] = value
 
     def look_turn(turn, carry):
         places = [(SIDE - 1 - turn) * SIDE + i for i in range(SIDE)]
@@ -476,6 +513,7 @@
             table,
             line,
             line,
+            pltpu.SemaphoreType.REGULAR,
             pltpu.SemaphoreType.DMA((6,)),
             pltpu.SemaphoreType.DMA((3,)),
             pltpu.SemaphoreType.DMA((3,)),

time: 48.5 us -> 42.5 us (0.88)
  Pallas kernels: 47.7 us -> 41.7 us
    pallas_call x1, Pallas kernels: 47 us -> 40.9 us  [body(): pl.pallas_call(step_kernel, out_shape=(vmem((PLANES, WIDTH, NY), F32), vm...]
where the time goes in v3:
time: 42.5 us; the launch traced here: 42.4 us
  Pallas kernels  41.7 us (98%)
  between operations  0.64 us (2%)
    pallas_call x1, Pallas kernels, body(): pl.pallas_call(step_kernel, out_shape=(vmem((PLANES, WIDTH, NY), F32), vm...  40.9 us

profile of v3, /device:TPU:0, one launch (start us, length us, event | category | flops | bytes accessed | tf_op | source)
XLA Modules:
  0.0 42.4 jit_solution(1190429945828530132)
XLA Ops:
  0.6 40.9 %shard_map.77 = (f32[16,16,256]{2,1,0:T(8,128)S(1)}, f32[3,128,128]{2,1,0:T(8,128)S(1)}) custom-call(f32[3,128,128]{2,1,0:T(8,128)} %velocity_in.1, f32[3,128,128]{2,1,0:T(8,128)} %noise_in.1, s32[128,128]{1,0:T(8,128)} %plane_in.1, s32[128,128]{1,0:T(8,128)} %column_in.1, s32[1,128]{1,0:T(1,128)} %bitcast.1, f32[16,16,256]{2,1,0:T(8,128)} %temp_in.1), custom_call_target="tpu_custom_call" | custom-call | tf_op jit(solution)/shard_map/pallas_call | solution.py:485
  41.6 0.8 %shard_map.78 = (f32[16,16,256]{2,1,0:T(8,128)}, f32[3,128,128]{2,1,0:T(8,128)}) custom-call(f32[16,16,256]{2,1,0:T(8,128)S(1)} %get-tuple-element.4.solved, f32[3,128,128]{2,1,0:T(8,128)S(1)} %get-tuple-element.5.moved), custom_call_target="tpu_custom_call" | custom-call | tf_op jit(solution)/shard_map/pallas_call | solution.py:524

commit v4 on v3

--- a/solution.py
+++ b/solution.py
@@ -135,16 +135,39 @@
         right.append(jnp.where(y_ids == spread, constant(1.0), constant(0.0)))
     hot = jnp.concatenate(right, axis=1)
     picked = dot(high_table, hot) + dot(low_table, hot)
-    out = []
-    for brick in range(BAND):
-        part = picked[:, brick * LANES : (brick + 1) * LANES].reshape(ROWS // 8, 8, LANES)
-        mine = jnp.broadcast_to(row[brick : brick + 1], (8, LANES))
-        for bit in (7, 6, 5, 4, 3):
-            half = part.shape[0] // 2
-            part = jnp.where(bit_of(mine, bit)[None], part[half:], part[:half])
-        hit = iota((8, LANES), 0) == (mine & 7)
-        out.append(jnp.sum(jnp.where(hit, part[0], 0.0), axis=0, keepdims=True))
-    return jnp.concatenate(out, axis=0)
+    tables = []
+    for start in range(0, picked.shape[0], ROWS):
+        out = []
+        for brick in range(BAND):
+            lanes = slice(brick * LANES, (brick + 1) * LANES)
+            part = picked[start : start + ROWS, lanes].reshape(ROWS // 8, 8, LANES)
+            mine = jnp.broadcast_to(row[brick : brick + 1], (8, LANES))
+            for bit in (7, 6, 5, 4, 3):
+                half = part.shape[0] // 2
+                part = jnp.where(bit_of(mine, bit)[None], part[half:], part[:half])
+            hit = iota((8, LANES), 0) == (mine & 7)
+            out.append(jnp.sum(jnp.where(hit, part[0], 0.0), axis=0, keepdims=True))
+        tables.append(jnp.concatenate(out, axis=0))
+    return tables
+
+
+def look_ends(ends, code):
+    row, y = decode(code)
+    lane, second = y % LANES, y >= LANES
+
+    def pick(values):
+        return jnp.take_along_axis(jnp.broadcast_to(values, (BAND, LANES)), lane, axis=1)
+
+    def tree(end, start, size):
+        if size == 1:
+            values = ends[start, end : end + 1, :]
+            return jnp.where(second, pick(values[:, LANES:]), pick(values[:, :LANES]))
+        half = size // 2
+        return jnp.where(
+            bit_of(row, half.bit_length() - 1), tree(end, start + half, half), tree(end, start, half)
+        )
+
+    return tree(0, 0, WIDTH), tree(1, 0, WIDTH)
 
 
 def look_lanes(table, code):
@@ -171,6 +194,7 @@
 WIDE_PEERS = [1, 2, 3]
 DEEP_PEERS = [SIDE, 2 * SIDE, 3 * SIDE]
 HOPS = [0, 1, 2, 1]
+EARLY = [12, 13, 14, 15]
 FAR_FIRST = sorted(range(1, SLABS), key=lambda p: -(HOPS[p // SIDE] + HOPS[p % SIDE]))
 
 
@@ -268,30 +292,52 @@
     ends[:, 1, :] = value
 
 
+def compose(fixed, to_low, to_high, high_parts, low_parts):
+    shape = (WIDTH, NY)
+    values = [jnp.zeros(shape, F32), jnp.zeros(shape, F32), jnp.ones(shape, F32)]
+    for p in range(PLANES - 1, -1, -1):
+        if p < PLANES - 1:
+            ratio = to_high[p]
+            values = [
+                fixed[p] + ratio * values[0],
+                to_low[p] + ratio * values[1],
+                ratio * values[2],
+            ]
+            fixed[p], to_low[p], to_high[p] = values
+        for number, value in enumerate(values):
+            rows = slice(number * ROWS + p * WIDTH, number * ROWS + (p + 1) * WIDTH)
+            high_parts[rows], low_parts[rows] = split2(value)
+
+
 def substitute(fixed, to_low, to_high, ends, solved, high_table, low_table):
     low_end = ends[:, 0, :]
-    value = ends[:, 1, :]
-    for p in range(PLANES - 1, -1, -1):
+    last = ends[:, 1, :]
+    for p in range(PLANES):
+        value = last
         if p < PLANES - 1:
-            value = (fixed[p] + to_low[p] * low_end) + to_high[p] * value
+            value = (fixed[p] + to_low[p] * low_end) + to_high[p] * last
         solved[p] = value
         high, low = split2(value)
         high_table[p * WIDTH : (p + 1) * WIDTH] = high
         low_table[p * WIDTH : (p + 1) * WIDTH] = low
 
 
-def kick(velocity, noise, count, slot, returned, moved):
+def kick_ready(velocity, count, slot, moved):
     used = used_mask(count[...])
-    slots = SLABS * SLOTS
-    slot_ids = iota((BRICKS, slots), 1).astype(F32)
+    slot_ids = iota((BRICKS, SLABS * SLOTS), 1).astype(F32)
     where_from = jnp.concatenate([slot[...], slot[...]], axis=1)
-    pick = jnp.where(slot_ids == where_from, 1.0, 0.0).astype(BF16)
-    high, middle, low = split3(returned[...].reshape(slots, LANES))
-    temp = (dot(pick, high) + dot(pick, middle)) + dot(pick, low)
+    for axis in range(3):
+        moved[axis] = jnp.where(used, (1.0 - KICK_RATE) * velocity[axis], 0.0)
+    return used, jnp.where(slot_ids == where_from, 1.0, 0.0).astype(BF16)
+
+
+def kick(noise, used, pick, returned, moved):
+    terms = jnp.concatenate(split3(returned[...].reshape(SLABS * SLOTS, LANES)), axis=1)
+    sums = dot(pick, terms)
+    temp = (sums[:, :LANES] + sums[:, LANES : 2 * LANES]) + sums[:, 2 * LANES :]
     scale = jnp.sqrt(2.0 * KICK_RATE * temp)
     for axis in range(3):
-        kicked = (1.0 - KICK_RATE) * velocity[axis] + scale * noise[axis]
-        moved[axis] = jnp.where(used, kicked, 0.0)
+        moved[axis] += jnp.where(used, scale * noise[axis], 0.0)
 
 
 def step_kernel(
@@ -299,7 +345,7 @@
     solved, moved,
     velocity, noise, plane, column, count, temp,
     send, got, slot, edges, below, sides, energies, counts, reduced, systems, ends, own_ends,
-    fixed, to_low, to_high, high_table, low_table, reply, returned,
+    fixed, to_low, to_high, high_table, low_table, high_parts, low_parts, parts, reply, returned,
     row_ready, load_sem, halo_send, halo_recv,
     atom_send, atom_recv, system_send, system_recv, end_send, end_recv, reply_send, reply_recv,
 ):
@@ -398,6 +444,19 @@
     for place in FAR_FIRST:
         system(place).start()
     systems[me] = reduced[me]
+    compose(fixed, to_low, to_high, high_parts, low_parts)
+
+    def look_early(places):
+        bands = [(place, band) for place in places for band in (0, BAND)]
+        values = [
+            look_product(high_parts[...], low_parts[...], got[place, 1][band : band + BAND])
+            for place, band in bands
+        ]
+        for (place, band), value in zip(bands, values):
+            for number in range(3):
+                parts[place - EARLY[0], number, band : band + BAND] = value[number]
+
+    look_early(EARLY[:2])
     for place in range(1, SLABS):
         system(place).wait_recv()
     solve_reduced(systems, ends)
@@ -411,6 +470,7 @@
     for place in FAR_FIRST:
         end(place).start()
     own_ends[me] = ends[me]
+    look_early(EARLY[2:])
     for place in range(1, SLABS):
         end(place).wait_recv()
     substitute(fixed, to_low, to_high, own_ends, solved, high_table, low_table)
@@ -421,34 +481,42 @@
             {"gz": behind(place)},
         )
 
-    def look_places(places, target):
+    def finish(place, band):
+        rows = slice(band, band + BAND)
+        below_end, last = look_ends(own_ends, got[place, 1][rows])
+        base, low, high = [parts[place - EARLY[0], number, rows] for number in range(3)]
+        return (base + low * below_end) + high * last
+
+    def look_places(places, target, products, early=()):
         bands = [(source, place, band) for source, place in places for band in (0, BAND)]
+        ends_of = [(place, band) for place in early for band in (0, BAND)]
+        done = [finish(place, band) for place, band in ends_of]
         values = []
         for number, (source, place, band) in enumerate(bands):
             code = source[place, 1][band : band + BAND]
-            if number * 8 < len(bands) * 5:
-                values.append(look_product(high_table[...], low_table[...], code))
+            if number < products:
+                values.append(look_product(high_table[...], low_table[...], code)[0])
             else:
                 values.append(look_lanes(solved, code))
+        for (place, band), value in zip(ends_of, done):
+            target[place, band : band + BAND] = value
         for (_, place, band), value in zip(bands, values):
             target[place, band : band + BAND] = value
 
-    def look_turn(turn, carry):
-        places = [(SIDE - 1 - turn) * SIDE + i for i in range(SIDE)]
-        look_places([(got, place) for place in places], reply)
-        for place in places:
+    def look_group(places, products, early=()):
+        look_places([(got, place) for place in places], reply, products, early)
+        for place in [*early, *places]:
             answer(place).start()
-        return carry
-
-    lax.fori_loop(0, SIDE - 1, look_turn, 0)
-    look_places([(got, place) for place in range(1, SIDE)], reply)
-    for place in range(1, SIDE):
-        answer(place).start()
-    look_places([(send, 0)], returned)
+
+    look_group(range(8, 12), 6, EARLY)
+    look_group(range(4, 8), 5)
+    look_group(range(1, 4), 4)
+    look_places([(send, 0)], returned, 2)
     loads[5].wait()
+    used, pick = kick_ready(velocity, count, slot, moved)
     for place in range(1, SLABS):
         answer(place).wait_recv()
-    kick(velocity, noise, count, slot, returned, moved)
+    kick(noise, used, pick, returned, moved)
     for halo in halos:
         halo.wait_send()
     for place in range(1, SLABS):
@@ -511,6 +579,9 @@
             inner,
             table,
             table,
+            vmem((3 * ROWS, NY), BF16),
+            vmem((3 * ROWS, NY), BF16),
+            vmem((len(EARLY), 3, SLOTS, LANES), F32),
             line,
             line,
             pltpu.SemaphoreType.REGULAR,

time: 42.5 us -> 41 us (0.965)
  Pallas kernels: 41.7 us -> 40.1 us
    pallas_call x1, Pallas kernels: 40.9 us -> 39.3 us  [body(): pl.pallas_call(step_kernel, out_shape=(vmem((PLANES, WIDTH, NY), F32), vm...]
where the time goes in v4:
time: 41 us; the launch traced here: 40.9 us
  Pallas kernels  40.1 us (98%)
  between operations  0.8 us (2%)
    pallas_call x1, Pallas kernels, body(): pl.pallas_call(step_kernel, out_shape=(vmem((PLANES, WIDTH, NY), F32), vm...  39.3 us

profile of v4, /device:TPU:0, one launch (start us, length us, event | category | flops | bytes accessed | tf_op | source)
XLA Modules:
  0.0 40.9 jit_solution(16573379612444104029)
XLA Ops:
  0.6 39.3 %shard_map.77 = (f32[16,16,256]{2,1,0:T(8,128)S(1)}, f32[3,128,128]{2,1,0:T(8,128)S(1)}) custom-call(f32[3,128,128]{2,1,0:T(8,128)} %velocity_in.1, f32[3,128,128]{2,1,0:T(8,128)} %noise_in.1, s32[128,128]{1,0:T(8,128)} %plane_in.1, s32[128,128]{1,0:T(8,128)} %column_in.1, s32[1,128]{1,0:T(1,128)} %bitcast.1, f32[16,16,256]{2,1,0:T(8,128)} %temp_in.1), custom_call_target="tpu_custom_call" | custom-call | tf_op jit(solution)/shard_map/pallas_call | solution.py:553
  39.9 0.8 %shard_map.78 = (f32[16,16,256]{2,1,0:T(8,128)}, f32[3,128,128]{2,1,0:T(8,128)}) custom-call(f32[16,16,256]{2,1,0:T(8,128)S(1)} %get-tuple-element.4.solved, f32[3,128,128]{2,1,0:T(8,128)S(1)} %get-tuple-element.5.moved), custom_call_target="tpu_custom_call" | custom-call | tf_op jit(solution)/shard_map/pallas_call | solution.py:595

commit v5 on v4

--- a/solution.py
+++ b/solution.py
@@ -427,10 +427,11 @@
     bin_places(range(1, SIDE))
 
     def bin_turn(turn, carry):
-        bin_places([turn * SIDE + i for i in range(SIDE)])
+        steps = 1 + 2 * turn - 3 * (turn * (turn - 1) // 2)
+        bin_places([steps * SIDE + i for i in range(SIDE)])
         return carry
 
-    lax.fori_loop(1, SIDE, bin_turn, 0)
+    lax.fori_loop(0, SIDE - 1, bin_turn, 0)
     for halo in halos:
         halo.wait_recv()
     eliminate(temp, below, sides.at[0], sides.at[1], me, energies, counts, reduced, fixed, to_low, to_high)

time: 41 us -> 41 us (level)
  no operation moved by 1% of the time
where the time goes in v5:
time: 41 us; the launch traced here: 40.9 us
  Pallas kernels  40.1 us (98%)
  between operations  0.8 us (2%)
    pallas_call x1, Pallas kernels, body(): pl.pallas_call(step_kernel, out_shape=(vmem((PLANES, WIDTH, NY), F32), vm...  39.3 us

profile of v5, /device:TPU:0, one launch (start us, length us, event | category | flops | bytes accessed | tf_op | source)
XLA Modules:
  0.0 40.9 jit_solution(9617887447034351471)
XLA Ops:
  0.6 39.3 %shard_map.77 = (f32[16,16,256]{2,1,0:T(8,128)S(1)}, f32[3,128,128]{2,1,0:T(8,128)S(1)}) custom-call(f32[3,128,128]{2,1,0:T(8,128)} %velocity_in.1, f32[3,128,128]{2,1,0:T(8,128)} %noise_in.1, s32[128,128]{1,0:T(8,128)} %plane_in.1, s32[128,128]{1,0:T(8,128)} %column_in.1, s32[1,128]{1,0:T(1,128)} %bitcast.1, f32[16,16,256]{2,1,0:T(8,128)} %temp_in.1), custom_call_target="tpu_custom_call" | custom-call | tf_op jit(solution)/shard_map/pallas_call | solution.py:554
  39.9 0.8 %shard_map.78 = (f32[16,16,256]{2,1,0:T(8,128)}, f32[3,128,128]{2,1,0:T(8,128)}) custom-call(f32[16,16,256]{2,1,0:T(8,128)S(1)} %get-tuple-element.4.solved, f32[3,128,128]{2,1,0:T(8,128)S(1)} %get-tuple-element.5.moved), custom_call_target="tpu_custom_call" | custom-call | tf_op jit(solution)/shard_map/pallas_call | solution.py:596
